TPU v7x, 256 devices: a whole 4x4x8 slice. The times are simulated.
256 devices in a mesh: scan: 64 (over x, y_hi, z), tile: 4 (over y_lo, core).
Axes of the slice: x: 4, y: 4 (y_hi: 2, y_lo: 2; y = y_hi * 2 + y_lo), z: 8, core: 2. Of those that a mesh axis runs over, the one named last changes fastest.
Arguments:
- probe_modes: float32 [3072, 256], P(('scan', 'tile')), may hold values from -2.1 to 2.1
- object_tiles: float32 [4, 2, 2, 320, 320], P('tile'), may hold values from -4 to 4
- scan_offsets: int32 [512, 2], P(('scan', 'tile')), may hold values from 0 to 64, as said below
- patch_tiles: int32 [512], P(('scan', 'tile')), may hold values from 0 to 3, as said below
- amplitudes: bfloat16 [512, 256, 256], P(('scan', 'tile')), may hold values from 0.5 to 20
Outputs:
- probe_gradient: float32 [3072, 256], P(('scan', 'tile'))
- object_gradient: float32 [4, 2, 2, 320, 320], P('tile', None, None, 'scan')
Inputs may be any that keep to these rules, and one draw needn't show every extreme that they name: `patch_tiles`: each entry names the tile that wholly holds the patch of its position. `scan_offsets`: every patch lies wholly inside its tile.
All inputs are finite; a program needn't handle non-finite values.
Results may differ from a plain program's by a relative error of at most 0.02.
Values sent between devices are 32-bit elements; how exact they have to be, the bound alone decides.
No kernel may reach another device: no remote copies, remote signals or barrier semaphores. Data moves between devices by JAX's collectives and lax.ppermute only.
A program may use at most 128 MiB of HBM per device.

v0:
```python
import math
import jax
import jax.numpy as jnp
from jax import lax
from jax.sharding import PartitionSpec as P


def complex_tables(pixels):
    pixel_index = jnp.arange(pixels, dtype=jnp.int32)
    offset = pixel_index[:, None] - pixel_index[None, :]
    chirp_phase = (offset * offset % (2 * pixels)).astype(jnp.float32) * (math.pi / pixels)
    product = (pixel_index[:, None] * pixel_index[None, :] % pixels).astype(jnp.float32) * (
        2.0 * math.pi / pixels
    )
    norm_scale = 1.0 / math.sqrt(pixels)
    fresnel = (jnp.stack([jnp.cos(chirp_phase), jnp.sin(chirp_phase)]) * norm_scale).astype(
        jnp.bfloat16
    )
    spectral = (jnp.stack([jnp.cos(product), -jnp.sin(product)]) * norm_scale).astype(jnp.bfloat16)
    return (fresnel, spectral)


def multiply_object(exit_wave, object_patch):
    real_part = exit_wave[0] * object_patch[0] - exit_wave[1] * object_patch[1]
    imag_part = exit_wave[0] * object_patch[1] + exit_wave[1] * object_patch[0]
    return jnp.stack([real_part, imag_part])


def left_side(matrix_part, component):
    return jnp.einsum("ij,mjk->mik", matrix_part, component, preferred_element_type=jnp.float32)


def right_side(component, matrix_part):
    return jnp.einsum("mik,jk->mij", component, matrix_part, preferred_element_type=jnp.float32)


def left_product(matrix, exit_wave):
    real_part = left_side(matrix[0], exit_wave[0]) - left_side(matrix[1], exit_wave[1])
    imag_part = left_side(matrix[0], exit_wave[1]) + left_side(matrix[1], exit_wave[0])
    return jnp.stack([real_part, imag_part])


def right_product(exit_wave, matrix):
    real_part = right_side(exit_wave[0], matrix[0]) - right_side(exit_wave[1], matrix[1])
    imag_part = right_side(exit_wave[0], matrix[1]) + right_side(exit_wave[1], matrix[0])
    return jnp.stack([real_part, imag_part])


def position_loss(probe_values, patch_values, amplitude, fresnel, spectral):
    exit_wave = probe_values
    layers = patch_values.shape[0]
    for slice_index in range(layers):
        exit_wave = multiply_object(exit_wave, patch_values[slice_index])
        matrix = fresnel if slice_index < layers - 1 else spectral
        rounded = exit_wave.astype(jnp.bfloat16)
        halfway = left_product(matrix, rounded).astype(jnp.bfloat16)
        exit_wave = right_product(halfway, matrix)
    intensity = jnp.sum(exit_wave * exit_wave, axis=(0, 1))
    residue = jnp.sqrt(intensity + 1.0) - amplitude.astype(jnp.float32)
    return jnp.sum(residue * residue)


def body(probe_modes, object_tiles, scan_offsets, patch_tiles, amplitudes):
    tile_count = lax.axis_size("tile")
    scan_count = lax.axis_size("scan")
    pixels = probe_modes.shape[1]
    layers = object_tiles.shape[1]
    side = object_tiles.shape[3]
    whole_probe = lax.all_gather(probe_modes, ("scan", "tile"), axis=0, tiled=True)
    probe_field = whole_probe.reshape(2, -1, pixels, pixels)
    fresnel, spectral = complex_tables(pixels)
    whole_object = lax.all_gather(object_tiles, "tile", axis=0, tiled=True)

    def cut_own(tile_number, corner):
        anchor = (tile_number, jnp.int32(0), jnp.int32(0), corner[0], corner[1])
        return lax.dynamic_slice(whole_object, anchor, (1, layers, 2, pixels, pixels))[0]

    own_patches = jax.vmap(cut_own)(patch_tiles, scan_offsets)

    def one_position(probe_total, inputs):
        object_patch, amplitude = inputs

        def local_loss(probe_values, patch_values):
            return position_loss(probe_values, patch_values, amplitude, fresnel, spectral)

        misfit, pullback = jax.vjp(local_loss, probe_field, object_patch)
        probe_part, patch_part = pullback(jnp.ones_like(misfit))
        return (probe_total + probe_part, patch_part)

    probe_total, patch_gradients = lax.scan(
        one_position, jnp.zeros_like(probe_field), (own_patches, amplitudes)
    )

    def add_patch(object_total, inputs):
        gradient_piece, tile_number, corner = inputs
        anchor = (tile_number, jnp.int32(0), jnp.int32(0), corner[0], corner[1])
        current = lax.dynamic_slice(object_total, anchor, (1,) + gradient_piece.shape)
        return (
            lax.dynamic_update_slice(object_total, current + gradient_piece[None], anchor),
            None,
        )

    whole_shape = (tile_count,) + object_tiles.shape[1:]
    object_total, _ = lax.scan(
        add_patch, jnp.zeros(whole_shape, jnp.float32), (patch_gradients, patch_tiles, scan_offsets)
    )
    row_count = side // scan_count
    arranged = object_total.reshape(tile_count, layers, 2, scan_count, row_count, side)
    arranged = arranged.transpose(3, 0, 1, 2, 4, 5).reshape(
        scan_count * tile_count, layers, 2, row_count, side
    )
    object_gradient = lax.psum_scatter(arranged, ("scan", "tile"), scatter_dimension=0, tiled=True)
    probe_gradient = lax.psum_scatter(
        probe_total.reshape(-1, pixels), ("scan", "tile"), scatter_dimension=0, tiled=True
    )
    return (probe_gradient, object_gradient)


def solution(mesh):
    placed = (
        P(("scan", "tile"), None),
        P("tile", None, None, None, None),
        P(("scan", "tile"), None),
        P(("scan", "tile")),
        P(("scan", "tile"), None, None),
    )
    return jax.shard_map(
        body,
        mesh=mesh,
        in_specs=placed,
        out_specs=(P(("scan", "tile"), None), P("tile", None, None, "scan", None)),
        check_vma=False,
    )
```

profile of v0, /device:TPU:6, one launch (start us, length us, event | category | flops | bytes accessed | tf_op | source)
XLA Modules:
  0.0 2013.1 jit_solution(5033408186173666694)
XLA Ops:
  12.0 415.8 %all-gather.6.cloned.1.call-done = f32[256,12,256]{2,1,0:T(8,128)} async-done(((f32[1,12,256]{2,1,0:T(8,128)}), f32[256,12,256]{2,1,0:T(8,128)}) %all-gather.6.cloned.1.call-update) | async-done | bytes 3145744 | tf_op jit(solution)/shard_map/all_gather | solution.py:69
  434.8 72.6 %all-gather.4.cloned.1.call-done = f32[4,2,2,320,320]{4,3,2,1,0:T(8,128)} async-done(((f32[1,2,2,320,320]{4,3,2,1,0:T(8,128)}), f32[4,2,2,320,320]{4,3,2,1,0:T(8,128)}) %all-gather.4.cloned.1.call-update) | async-done | bytes 6553616 | tf_op jit(solution)/shard_map/all_gather | solution.py:72
  518.1 107.1 %while.26 = (s32[]{:T(128)}, f32[2,6,256,256]{2,3,1,0:T(8,128)}, f32[2,2,2,256,256]{4,3,2,1,0:T(8,128)}, f32[2,6,256,256]{2,3,1,0:T(8,128)S(1)}, f32[2,2,2,256,2...) while((s32[]{:T(128)}, f32[2,6,256,256]{2,3,1,0:T(8,128)}, ...), condition=%wide.region_10.11_spmd.clone, body=%wide.region_0.10_spmd.clone.sunk | while | flops 6493634560 | bytes 218235760 | solution.py:90
  630.9 202.0 %while.24 = (s32[]{:T(128)}, f32[4,2,2,320,320]{4,2,3,1,0:T(2,128)}, s32[2]{0:T(128)S(1)}, s32[2,2]{1,0:T(2,128)S(1)}, f32[2,2,2,256,256]{4,3,2,1,0:T(8,128)}, /*index=5*/s32[]{:T(128)}, s32[]{:T(128)}, s32[]{:T(128)}, s32[]{:T(128)}) while((s32[]{:T(128)}, f32[4,2,2,320,320]{4,2,3,1,0:T(2,128)}, s32[2]{0:T(128)S(1)}, ...), condition=%wide.region_13.14_spmd, body=%wide.region_12.13_spmd.sunk | while | flops 262155 | bytes 9437447 | solution.py:104
  642.7 89.2 %dynamic_update_slice.11 = f32[4,2,2,320,320]{4,2,3,1,0:T(2,128)} dynamic-update-slice(f32[4,2,2,320,320]{4,2,3,1,0:T(2,128)} %get-tuple-element.452, f32[1,2,2,256,256]{4,2,3,1,0:T(2,128)S(1)} %copy.201, s32[]{:T(128)S(6)} %select_n.91, s32[]{:T(128)} %constant.64.clone.1..sunk, s32[]{:T(128)} %constant.64.clone.1..sunk, s32[]{:T(128)S(6)} %select_n.92, s32[]{:T(128)S(6)} %select_n.93) | dynamic-update-slice | bytes 2097156 | tf_op jit(solution)/shard_map/while/body/eval_jaxpr/dynamic_update_slice | solution.py:99
  743.7 89.2 %dynamic_update_slice.11 = f32[4,2,2,320,320]{4,2,3,1,0:T(2,128)} dynamic-update-slice(f32[4,2,2,320,320]{4,2,3,1,0:T(2,128)} %get-tuple-element.452, f32[1,2,2,256,256]{4,2,3,1,0:T(2,128)S(1)} %copy.201, s32[]{:T(128)S(6)} %select_n.91, s32[]{:T(128)} %constant.64.clone.1..sunk, s32[]{:T(128)} %constant.64.clone.1..sunk, s32[]{:T(128)S(6)} %select_n.92, s32[]{:T(128)S(6)} %select_n.93) | dynamic-update-slice | bytes 2097156 | tf_op jit(solution)/shard_map/while/body/eval_jaxpr/dynamic_update_slice | solution.py:99
  846.2 592.8 %fusion = f32[16,256]{1,0:T(8,128)S(1)} fusion(f32[3072,256]{1,0:T(8,128)} %bitcast.555), kind=kCustom, calls=%all-reduce-scatter | all-reduce-scatter fusion | flops 1048577 | bytes 3162112
  1439.0 79.9 %collective-permute-start = (f32[16,256]{1,0:T(8,128)S(1)}, f32[16,256]{1,0:T(8,128)S(1)}, u32[]{:S(2)}, u32[]{:S(2)}) collective-permute-start(f32[16,256]{1,0:T(8,128)S(1)} %fusion), channel_id=1, source_target_pairs={{0,1},{1,2},{2,3},{3,4},{4,5},{5,6},{6,7},{7,8},{8,9},{9,10},{10,1... | collective-permute-start | bytes 49160
  1519.0 13.2 collective-permute-start.1
  1532.2 13.1 collective-permute-start.10
  1546.6 14.9 collective-permute-start.11
  1561.6 13.1 collective-permute-start.12
  1574.7 13.1 collective-permute-start.13
  1587.9 13.1 collective-permute-start.14
  1601.0 13.1 collective-permute-start.15
  1614.2 13.1 collective-permute-start.16
  1627.3 13.1 collective-permute-start.17
  1640.4 13.1 collective-permute-start.18
  1653.6 13.1 collective-permute-start.19
  1666.7 13.1 collective-permute-start.2
  1679.8 13.1 collective-permute-start.20
  1831.5 17.7 collective-permute-start.4
  1877.0 20.8 %collective-permute-start.5 = (f32[16,256]{1,0:T(8,128)S(1)}, f32[16,256]{1,0:T(8,128)S(1)}, u32[]{:S(2)}, u32[]{:S(2)}) collective-permute-start(f32[16,256]{1,0:T(8,128)S(1)} %fusion), channel_id=1, source_target_pairs={{0,6},{1,7},{2,8},{3,9},{4,10},{5,11},{6,12},{7,13},{8,14},{9,15},... | collective-permute-start | bytes 49160
  1925.8 13.3 collective-permute-start.6
  (311 shorter events, 423.8 us)
Async XLA Ops:
  7.2 420.6 %all-gather.6.cloned.1.call-start = ((), (), s32[]{:S(2)}) async-start(), calls=%async_computation.1 | async-start | bytes 4210688 | tf_op jit(solution)/shard_map/all_gather | solution.py:69
  7.9 499.4 %all-gather.4.cloned.1.call-start = ((), (), s32[]{:S(2)}) async-start(), calls=%async_computation | async-start | bytes 9830400 | tf_op jit(solution)/shard_map/all_gather | solution.py:72
  8.7 1996.3 %all-reduce.39.cloned.1.call-start = ((), (), s32[]{:S(2)}) async-start(), calls=%async_computation.2 | async-start | bytes 15728640
  1439.0 135.7 %collective-permute-start = (f32[16,256]{1,0:T(8,128)S(1)}, f32[16,256]{1,0:T(8,128)S(1)}, u32[]{:S(2)}, u32[]{:S(2)}) collective-permute-start(f32[16,256]{1,0:T(8,128)S(1)} %fusion), channel_id=1, source_target_pairs={{0,1},{1,2},{2,3},{3,4},{4,5},{5,6},{6,7},{7,8},{8,9},{9,10},{10,1... | collective-permute-start | bytes 49160
  1519.0 68.9 %collective-permute-start.1 = (f32[16,256]{1,0:T(8,128)S(1)}, f32[16,256]{1,0:T(8,128)S(1)}, u32[]{:S(2)}, u32[]{:S(2)}) collective-permute-start(f32[16,256]{1,0:T(8,128)S(1)} %fusion), channel_id=1, source_target_pairs={{0,2},{1,3},{2,4},{3,5},{4,6},{5,7},{6,8},{7,9},{8,10},{9,11},{10,... | collective-permute-start | bytes 49160
  1532.2 68.8 %collective-permute-start.10 = (f32[16,256]{1,0:T(8,128)S(1)}, f32[16,256]{1,0:T(8,128)S(1)}, u32[]{:S(2)}, u32[]{:S(2)}) collective-permute-start(f32[16,256]{1,0:T(8,128)S(1)} %fusion), channel_id=1, source_target_pairs={{0,11},{1,12},{2,13},{3,14},{4,15},{5,16},{6,17},{7,18},{8,19},{9,... | collective-permute-start | bytes 49160
  1546.6 67.5 %collective-permute-start.11 = (f32[16,256]{1,0:T(8,128)S(1)}, f32[16,256]{1,0:T(8,128)S(1)}, u32[]{:S(2)}, u32[]{:S(2)}) collective-permute-start(f32[16,256]{1,0:T(8,128)S(1)} %fusion), channel_id=1, source_target_pairs={{0,12},{1,13},{2,14},{3,15},{4,16},{5,17},{6,18},{7,19},{8,20},{9,... | collective-permute-start | bytes 49160
  1561.6 65.7 %collective-permute-start.12 = (f32[16,256]{1,0:T(8,128)S(1)}, f32[16,256]{1,0:T(8,128)S(1)}, u32[]{:S(2)}, u32[]{:S(2)}) collective-permute-start(f32[16,256]{1,0:T(8,128)S(1)} %fusion), channel_id=1, source_target_pairs={{0,13},{1,14},{2,15},{3,16},{4,17},{5,18},{6,19},{7,20},{8,21},{9,... | collective-permute-start | bytes 49160
  1574.7 65.7 %collective-permute-start.13 = (f32[16,256]{1,0:T(8,128)S(1)}, f32[16,256]{1,0:T(8,128)S(1)}, u32[]{:S(2)}, u32[]{:S(2)}) collective-permute-start(f32[16,256]{1,0:T(8,128)S(1)} %fusion), channel_id=1, source_target_pairs={{0,14},{1,15},{2,16},{3,17},{4,18},{5,19},{6,20},{7,21},{8,22},{9,... | collective-permute-start | bytes 49160
  1587.9 65.7 %collective-permute-start.14 = (f32[16,256]{1,0:T(8,128)S(1)}, f32[16,256]{1,0:T(8,128)S(1)}, u32[]{:S(2)}, u32[]{:S(2)}) collective-permute-start(f32[16,256]{1,0:T(8,128)S(1)} %fusion), channel_id=1, source_target_pairs={{0,15},{1,16},{2,17},{3,18},{4,19},{5,20},{6,21},{7,22},{8,23},{9,... | collective-permute-start | bytes 49160
  1601.0 65.7 %collective-permute-start.15 = (f32[16,256]{1,0:T(8,128)S(1)}, f32[16,256]{1,0:T(8,128)S(1)}, u32[]{:S(2)}, u32[]{:S(2)}) collective-permute-start(f32[16,256]{1,0:T(8,128)S(1)} %fusion), channel_id=1, source_target_pairs={{0,16},{1,17},{2,18},{3,19},{4,20},{5,21},{6,22},{7,23},{8,24},{9,... | collective-permute-start | bytes 49160
  1614.2 65.7 %collective-permute-start.16 = (f32[16,256]{1,0:T(8,128)S(1)}, f32[16,256]{1,0:T(8,128)S(1)}, u32[]{:S(2)}, u32[]{:S(2)}) collective-permute-start(f32[16,256]{1,0:T(8,128)S(1)} %fusion), channel_id=1, source_target_pairs={{0,17},{1,18},{2,19},{3,20},{4,21},{5,22},{6,23},{7,24},{8,25},{9,... | collective-permute-start | bytes 49160
  1627.3 65.7 %collective-permute-start.17 = (f32[16,256]{1,0:T(8,128)S(1)}, f32[16,256]{1,0:T(8,128)S(1)}, u32[]{:S(2)}, u32[]{:S(2)}) collective-permute-start(f32[16,256]{1,0:T(8,128)S(1)} %fusion), channel_id=1, source_target_pairs={{0,18},{1,19},{2,20},{3,21},{4,22},{5,23},{6,24},{7,25},{8,26},{9,... | collective-permute-start | bytes 49160
  1640.4 65.7 %collective-permute-start.18 = (f32[16,256]{1,0:T(8,128)S(1)}, f32[16,256]{1,0:T(8,128)S(1)}, u32[]{:S(2)}, u32[]{:S(2)}) collective-permute-start(f32[16,256]{1,0:T(8,128)S(1)} %fusion), channel_id=1, source_target_pairs={{0,19},{1,20},{2,21},{3,22},{4,23},{5,24},{6,25},{7,26},{8,27},{9,... | collective-permute-start | bytes 49160
  1653.6 65.7 %collective-permute-start.19 = (f32[16,256]{1,0:T(8,128)S(1)}, f32[16,256]{1,0:T(8,128)S(1)}, u32[]{:S(2)}, u32[]{:S(2)}) collective-permute-start(f32[16,256]{1,0:T(8,128)S(1)} %fusion), channel_id=1, source_target_pairs={{0,20},{1,21},{2,22},{3,23},{4,24},{5,25},{6,26},{7,27},{8,28},{9,... | collective-permute-start | bytes 49160
  1666.7 65.7 %collective-permute-start.2 = (f32[16,256]{1,0:T(8,128)S(1)}, f32[16,256]{1,0:T(8,128)S(1)}, u32[]{:S(2)}, u32[]{:S(2)}) collective-permute-start(f32[16,256]{1,0:T(8,128)S(1)} %fusion), channel_id=1, source_target_pairs={{0,3},{1,4},{2,5},{3,6},{4,7},{5,8},{6,9},{7,10},{8,11},{9,12},{10... | collective-permute-start | bytes 49160
  1679.8 65.7 %collective-permute-start.20 = (f32[16,256]{1,0:T(8,128)S(1)}, f32[16,256]{1,0:T(8,128)S(1)}, u32[]{:S(2)}, u32[]{:S(2)}) collective-permute-start(f32[16,256]{1,0:T(8,128)S(1)} %fusion), channel_id=1, source_target_pairs={{0,21},{1,22},{2,23},{3,24},{4,25},{5,26},{6,27},{7,28},{8,29},{9,... | collective-permute-start | bytes 49160
  1693.0 65.7 %collective-permute-start.21 = (f32[16,256]{1,0:T(8,128)S(1)}, f32[16,256]{1,0:T(8,128)S(1)}, u32[]{:S(2)}, u32[]{:S(2)}) collective-permute-start(f32[16,256]{1,0:T(8,128)S(1)} %fusion), channel_id=1, source_target_pairs={{0,22},{1,23},{2,24},{3,25},{4,26},{5,27},{6,28},{7,29},{8,30},{9,... | collective-permute-start | bytes 49160
  1706.1 65.7 %collective-permute-start.22 = (f32[16,256]{1,0:T(8,128)S(1)}, f32[16,256]{1,0:T(8,128)S(1)}, u32[]{:S(2)}, u32[]{:S(2)}) collective-permute-start(f32[16,256]{1,0:T(8,128)S(1)} %fusion), channel_id=1, source_target_pairs={{0,23},{1,24},{2,25},{3,26},{4,27},{5,28},{6,29},{7,30},{8,31},{9,... | collective-permute-start | bytes 49160
  1719.3 65.7 %collective-permute-start.23 = (f32[16,256]{1,0:T(8,128)S(1)}, f32[16,256]{1,0:T(8,128)S(1)}, u32[]{:S(2)}, u32[]{:S(2)}) collective-permute-start(f32[16,256]{1,0:T(8,128)S(1)} %fusion), channel_id=1, source_target_pairs={{0,24},{1,25},{2,26},{3,27},{4,28},{5,29},{6,30},{7,31},{8,32},{9,... | collective-permute-start | bytes 49160
  1732.4 58.7 %collective-permute-start.24 = (f32[16,256]{1,0:T(8,128)S(1)}, f32[16,256]{1,0:T(8,128)S(1)}, u32[]{:S(2)}, u32[]{:S(2)}) collective-permute-start(f32[16,256]{1,0:T(8,128)S(1)} %fusion), channel_id=1, source_target_pairs={{0,25},{1,26},{2,27},{3,28},{4,29},{5,30},{6,31},{7,32},{8,33},{9,... | collective-permute-start | bytes 49160
  1745.5 50.6 %collective-permute-start.25 = (f32[16,256]{1,0:T(8,128)S(1)}, f32[16,256]{1,0:T(8,128)S(1)}, u32[]{:S(2)}, u32[]{:S(2)}) collective-permute-start(f32[16,256]{1,0:T(8,128)S(1)} %fusion), channel_id=1, source_target_pairs={{0,26},{1,27},{2,28},{3,29},{4,30},{5,31},{6,32},{7,33},{8,34},{9,... | collective-permute-start | bytes 49160
  1758.7 46.2 %collective-permute-start.26 = (f32[16,256]{1,0:T(8,128)S(1)}, f32[16,256]{1,0:T(8,128)S(1)}, u32[]{:S(2)}, u32[]{:S(2)}) collective-permute-start(f32[16,256]{1,0:T(8,128)S(1)} %fusion), channel_id=1, source_target_pairs={{0,27},{1,28},{2,29},{3,30},{4,31},{5,32},{6,33},{7,34},{8,35},{9,... | collective-permute-start | bytes 49160
  1771.8 40.1 %collective-permute-start.27 = (f32[16,256]{1,0:T(8,128)S(1)}, f32[16,256]{1,0:T(8,128)S(1)}, u32[]{:S(2)}, u32[]{:S(2)}) collective-permute-start(f32[16,256]{1,0:T(8,128)S(1)} %fusion), channel_id=1, source_target_pairs={{0,28},{1,29},{2,30},{3,31},{4,32},{5,33},{6,34},{7,35},{8,36},{9,... | collective-permute-start | bytes 49160
  (64 other events, 1027.9 us)
Sparse Core Ops, SparseCore 0:
  9.9 417.8 all-gather.5
  429.6 77.6 all-gather.3
  842.1 281.0 all-reduce.38
where the time goes:
time: 2020 us; the launch traced here: 2010 us
  blocking collectives  593 us (29%)
  starting transfers between devices  546 us (27%)
  waiting for transfers between devices  501 us (25%)
  local copies, waits for them, and re-layouts  264 us (13%)
  other arithmetic  47 us (2%)
  matrix products  26.4 us (1%)
  loops' own time  21.1 us (1%)
    unnamed x1, blocking collectives  593 us
    unnamed x65, starting transfers between devices  546 us
    all_gather x1, waiting for transfers between devices, body(): lax.all_gather(probe_modes, ('scan', 'tile'), axis=0, tiled=True)  416 us
    dynamic_update_slice x4, local copies, waits for them, and re-layouts, add_patch(): lax.dynamic_update_slice(object_total, current + gradient_piece[None], an...  180 us
    all_gather x1, waiting for transfers between devices, body(): whole_object = lax.all_gather(object_tiles, 'tile', axis=0, tiled=True)  72.6 us
  transfers between devices with their start and end apart: 67, of which 4 were waited for; matrix products, arithmetic and copies ran while one was open for 30% of the time, Pallas kernels for 0%

commit v1 on v0

--- a/solution.py
+++ b/solution.py
@@ -66,7 +66,12 @@
     pixels = probe_modes.shape[1]
     layers = object_tiles.shape[1]
     side = object_tiles.shape[3]
-    whole_probe = lax.all_gather(probe_modes, ("scan", "tile"), axis=0, tiled=True)
+    whole_probe = jnp.concatenate(
+        lax.all_to_all(
+            jnp.stack([probe_modes] * lax.axis_size(("scan", "tile"))), ("scan", "tile"), 0, 0
+        ),
+        axis=0,
+    )
     probe_field = whole_probe.reshape(2, -1, pixels, pixels)
     fresnel, spectral = complex_tables(pixels)
     whole_object = lax.all_gather(object_tiles, "tile", axis=0, tiled=True)

time: 2020 us -> 1650 us (0.82)
  waiting for transfers between devices: 501 us -> 110 us
    all_gather x1 -> x0, waiting for transfers between devices: 416 us -> none  [body(): lax.all_gather(probe_modes, ('scan', 'tile'), axis=0, tiled=True)]
    all_to_all x0 -> x1, waiting for transfers between devices: none -> 92.4 us  [body(): lax.all_to_all(jnp.stack([probe_modes] * lax.axis_size(('scan', 'tile')))...]
    all_gather x1, waiting for transfers between devices: 72.6 us -> 5.89 us  [body(): whole_object = lax.all_gather(object_tiles, 'tile', axis=0, tiled=True)]
  transfers between devices with their start and end apart: 67 -> 67, of which waited for: 4 -> 4; matrix products, arithmetic and copies ran while one was open for 30% -> 38% of each run, Pallas kernels for 0% -> 0%
where the time goes in v1:
time: 1650 us; the launch traced here: 1640 us
  blocking collectives  592 us (36%)
  starting transfers between devices  562 us (34%)
  local copies, waits for them, and re-layouts  266 us (16%)
  waiting for transfers between devices  110 us (7%)
  other arithmetic  47.2 us (3%)
  matrix products  26.4 us (2%)
  loops' own time  21.1 us (1%)
    unnamed x1, blocking collectives  592 us
    unnamed x65, starting transfers between devices  546 us
    dynamic_update_slice x4, local copies, waits for them, and re-layouts, add_patch(): lax.dynamic_update_slice(object_total, current + gradient_piece[None], an...  180 us
    all_to_all x1, waiting for transfers between devices, body(): lax.all_to_all(jnp.stack([probe_modes] * lax.axis_size(('scan', 'tile')))...  92.4 us
  transfers between devices with their start and end apart: 67, of which 4 were waited for; matrix products, arithmetic and copies ran while one was open for 38% of the time, Pallas kernels for 0%

profile of v1, /device:TPU:6, one launch (start us, length us, event | category | flops | bytes accessed | tf_op | source)
XLA Modules:
  0.0 1640.0 jit_solution(7232989515708015356)
XLA Ops:
  10.4 15.6 all-to-all-start
  29.4 92.4 %all-to-all-done = f32[256,12,256]{2,1,0:T(8,128)} async-done(((f32[256,12,256]{2,1,0:T(8,128)}), f32[256,12,256]{2,1,0:T(8,128)}, u32[]{:S(2)}, u32[]{:S(2)}) %all-to-all-start) | async-done | bytes 3145760 | tf_op jit(solution)/shard_map/all_to_all | solution.py:70
  145.3 107.2 %while.26 = (s32[]{:T(128)}, f32[2,6,256,256]{2,3,1,0:T(8,128)}, f32[2,2,2,256,256]{4,3,2,1,0:T(8,128)}, f32[2,6,256,256]{2,3,1,0:T(8,128)S(1)}, f32[2,2,2,256,2...) while((s32[]{:T(128)}, f32[2,6,256,256]{2,3,1,0:T(8,128)}, ...), condition=%wide.region_10.11_spmd.clone, body=%wide.region_0.10_spmd.clone.sunk | while | flops 6493634560 | bytes 218235760 | solution.py:95
  258.1 202.0 %while.24 = (s32[]{:T(128)}, f32[4,2,2,320,320]{4,2,3,1,0:T(2,128)}, s32[2]{0:T(128)S(1)}, s32[2,2]{1,0:T(2,128)S(1)}, f32[2,2,2,256,256]{4,3,2,1,0:T(8,128)}, /*index=5*/s32[]{:T(128)}, s32[]{:T(128)}, s32[]{:T(128)}, s32[]{:T(128)}) while((s32[]{:T(128)}, f32[4,2,2,320,320]{4,2,3,1,0:T(2,128)}, s32[2]{0:T(128)S(1)}, ...), condition=%wide.region_13.14_spmd, body=%wide.region_12.13_spmd.sunk | while | flops 262155 | bytes 9437447 | solution.py:109
  269.9 89.2 %dynamic_update_slice.11 = f32[4,2,2,320,320]{4,2,3,1,0:T(2,128)} dynamic-update-slice(f32[4,2,2,320,320]{4,2,3,1,0:T(2,128)} %get-tuple-element.452, f32[1,2,2,256,256]{4,2,3,1,0:T(2,128)S(1)} %copy.201, s32[]{:T(128)S(6)} %select_n.91, s32[]{:T(128)} %constant.64.clone.1..sunk, s32[]{:T(128)} %constant.64.clone.1..sunk, s32[]{:T(128)S(6)} %select_n.92, s32[]{:T(128)S(6)} %select_n.93) | dynamic-update-slice | bytes 2097156 | tf_op jit(solution)/shard_map/while/body/eval_jaxpr/dynamic_update_slice | solution.py:104
  370.9 89.3 %dynamic_update_slice.11 = f32[4,2,2,320,320]{4,2,3,1,0:T(2,128)} dynamic-update-slice(f32[4,2,2,320,320]{4,2,3,1,0:T(2,128)} %get-tuple-element.452, f32[1,2,2,256,256]{4,2,3,1,0:T(2,128)S(1)} %copy.201, s32[]{:T(128)S(6)} %select_n.91, s32[]{:T(128)} %constant.64.clone.1..sunk, s32[]{:T(128)} %constant.64.clone.1..sunk, s32[]{:T(128)S(6)} %select_n.92, s32[]{:T(128)S(6)} %select_n.93) | dynamic-update-slice | bytes 2097156 | tf_op jit(solution)/shard_map/while/body/eval_jaxpr/dynamic_update_slice | solution.py:104
  473.4 592.2 %fusion = f32[16,256]{1,0:T(8,128)S(1)} fusion(f32[3072,256]{1,0:T(8,128)} %bitcast.554), kind=kCustom, calls=%all-reduce-scatter | all-reduce-scatter fusion | flops 1048577 | bytes 3162112
  1065.6 79.9 %collective-permute-start = (f32[16,256]{1,0:T(8,128)S(1)}, f32[16,256]{1,0:T(8,128)S(1)}, u32[]{:S(2)}, u32[]{:S(2)}) collective-permute-start(f32[16,256]{1,0:T(8,128)S(1)} %fusion), channel_id=1, source_target_pairs={{0,1},{1,2},{2,3},{3,4},{4,5},{5,6},{6,7},{7,8},{8,9},{9,10},{10,1... | collective-permute-start | bytes 49160
  1145.6 13.2 collective-permute-start.1
  1158.8 13.1 collective-permute-start.10
  1173.3 14.9 collective-permute-start.11
  1188.2 13.1 collective-permute-start.12
  1201.3 13.1 collective-permute-start.13
  1214.5 13.1 collective-permute-start.14
  1227.6 13.1 collective-permute-start.15
  1240.8 13.1 collective-permute-start.16
  1253.9 13.1 collective-permute-start.17
  1267.0 13.1 collective-permute-start.18
  1280.2 13.1 collective-permute-start.19
  1293.3 13.1 collective-permute-start.2
  1306.5 13.1 collective-permute-start.20
  1458.2 17.7 %collective-permute-start.4 = (f32[16,256]{1,0:T(8,128)S(1)}, f32[16,256]{1,0:T(8,128)S(1)}, u32[]{:S(2)}, u32[]{:S(2)}) collective-permute-start(f32[16,256]{1,0:T(8,128)S(1)} %fusion), channel_id=1, source_target_pairs={{0,5},{1,6},{2,7},{3,8},{4,9},{5,10},{6,11},{7,12},{8,13},{9,14},{... | collective-permute-start | bytes 49160
  1503.6 20.8 %collective-permute-start.5 = (f32[16,256]{1,0:T(8,128)S(1)}, f32[16,256]{1,0:T(8,128)S(1)}, u32[]{:S(2)}, u32[]{:S(2)}) collective-permute-start(f32[16,256]{1,0:T(8,128)S(1)} %fusion), channel_id=1, source_target_pairs={{0,6},{1,7},{2,8},{3,9},{4,10},{5,11},{6,12},{7,13},{8,14},{9,15},... | collective-permute-start | bytes 49160
  1552.4 13.3 collective-permute-start.6
  (313 shorter events, 431.2 us)
Async XLA Ops:
  7.2 127.5 %all-gather.2.cloned.1.call-start = ((), (), s32[]{:S(2)}) async-start(), calls=%async_computation.1 | async-start | bytes 9830400 | tf_op jit(solution)/shard_map/all_gather | solution.py:77
  10.4 111.4 %all-to-all-start = ((f32[256,12,256]{2,1,0:T(8,128)}), f32[256,12,256]{2,1,0:T(8,128)}, u32[]{:S(2)}, u32[]{:S(2)}) async-start(f32[256,12,256]{2,1,0:T(8,128)} %stack.22), calls=%async_computation | async-start | bytes 8388608 | tf_op jit(solution)/shard_map/all_to_all | solution.py:70
  26.0 1605.6 %all-reduce.39.cloned.1.call-start = ((), (), s32[]{:S(2)}) async-start(), calls=%async_computation.2 | async-start | bytes 15728640
  1065.6 135.7 %collective-permute-start = (f32[16,256]{1,0:T(8,128)S(1)}, f32[16,256]{1,0:T(8,128)S(1)}, u32[]{:S(2)}, u32[]{:S(2)}) collective-permute-start(f32[16,256]{1,0:T(8,128)S(1)} %fusion), channel_id=1, source_target_pairs={{0,1},{1,2},{2,3},{3,4},{4,5},{5,6},{6,7},{7,8},{8,9},{9,10},{10,1... | collective-permute-start | bytes 49160
  1145.6 68.9 %collective-permute-start.1 = (f32[16,256]{1,0:T(8,128)S(1)}, f32[16,256]{1,0:T(8,128)S(1)}, u32[]{:S(2)}, u32[]{:S(2)}) collective-permute-start(f32[16,256]{1,0:T(8,128)S(1)} %fusion), channel_id=1, source_target_pairs={{0,2},{1,3},{2,4},{3,5},{4,6},{5,7},{6,8},{7,9},{8,10},{9,11},{10,... | collective-permute-start | bytes 49160
  1158.8 68.8 %collective-permute-start.10 = (f32[16,256]{1,0:T(8,128)S(1)}, f32[16,256]{1,0:T(8,128)S(1)}, u32[]{:S(2)}, u32[]{:S(2)}) collective-permute-start(f32[16,256]{1,0:T(8,128)S(1)} %fusion), channel_id=1, source_target_pairs={{0,11},{1,12},{2,13},{3,14},{4,15},{5,16},{6,17},{7,18},{8,19},{9,... | collective-permute-start | bytes 49160
  1173.3 67.5 %collective-permute-start.11 = (f32[16,256]{1,0:T(8,128)S(1)}, f32[16,256]{1,0:T(8,128)S(1)}, u32[]{:S(2)}, u32[]{:S(2)}) collective-permute-start(f32[16,256]{1,0:T(8,128)S(1)} %fusion), channel_id=1, source_target_pairs={{0,12},{1,13},{2,14},{3,15},{4,16},{5,17},{6,18},{7,19},{8,20},{9,... | collective-permute-start | bytes 49160
  1188.2 65.7 %collective-permute-start.12 = (f32[16,256]{1,0:T(8,128)S(1)}, f32[16,256]{1,0:T(8,128)S(1)}, u32[]{:S(2)}, u32[]{:S(2)}) collective-permute-start(f32[16,256]{1,0:T(8,128)S(1)} %fusion), channel_id=1, source_target_pairs={{0,13},{1,14},{2,15},{3,16},{4,17},{5,18},{6,19},{7,20},{8,21},{9,... | collective-permute-start | bytes 49160
  1201.3 65.7 %collective-permute-start.13 = (f32[16,256]{1,0:T(8,128)S(1)}, f32[16,256]{1,0:T(8,128)S(1)}, u32[]{:S(2)}, u32[]{:S(2)}) collective-permute-start(f32[16,256]{1,0:T(8,128)S(1)} %fusion), channel_id=1, source_target_pairs={{0,14},{1,15},{2,16},{3,17},{4,18},{5,19},{6,20},{7,21},{8,22},{9,... | collective-permute-start | bytes 49160
  1214.5 65.7 %collective-permute-start.14 = (f32[16,256]{1,0:T(8,128)S(1)}, f32[16,256]{1,0:T(8,128)S(1)}, u32[]{:S(2)}, u32[]{:S(2)}) collective-permute-start(f32[16,256]{1,0:T(8,128)S(1)} %fusion), channel_id=1, source_target_pairs={{0,15},{1,16},{2,17},{3,18},{4,19},{5,20},{6,21},{7,22},{8,23},{9,... | collective-permute-start | bytes 49160
  1227.6 65.7 %collective-permute-start.15 = (f32[16,256]{1,0:T(8,128)S(1)}, f32[16,256]{1,0:T(8,128)S(1)}, u32[]{:S(2)}, u32[]{:S(2)}) collective-permute-start(f32[16,256]{1,0:T(8,128)S(1)} %fusion), channel_id=1, source_target_pairs={{0,16},{1,17},{2,18},{3,19},{4,20},{5,21},{6,22},{7,23},{8,24},{9,... | collective-permute-start | bytes 49160
  1240.8 65.7 %collective-permute-start.16 = (f32[16,256]{1,0:T(8,128)S(1)}, f32[16,256]{1,0:T(8,128)S(1)}, u32[]{:S(2)}, u32[]{:S(2)}) collective-permute-start(f32[16,256]{1,0:T(8,128)S(1)} %fusion), channel_id=1, source_target_pairs={{0,17},{1,18},{2,19},{3,20},{4,21},{5,22},{6,23},{7,24},{8,25},{9,... | collective-permute-start | bytes 49160
  1253.9 65.7 %collective-permute-start.17 = (f32[16,256]{1,0:T(8,128)S(1)}, f32[16,256]{1,0:T(8,128)S(1)}, u32[]{:S(2)}, u32[]{:S(2)}) collective-permute-start(f32[16,256]{1,0:T(8,128)S(1)} %fusion), channel_id=1, source_target_pairs={{0,18},{1,19},{2,20},{3,21},{4,22},{5,23},{6,24},{7,25},{8,26},{9,... | collective-permute-start | bytes 49160
  1267.0 65.7 %collective-permute-start.18 = (f32[16,256]{1,0:T(8,128)S(1)}, f32[16,256]{1,0:T(8,128)S(1)}, u32[]{:S(2)}, u32[]{:S(2)}) collective-permute-start(f32[16,256]{1,0:T(8,128)S(1)} %fusion), channel_id=1, source_target_pairs={{0,19},{1,20},{2,21},{3,22},{4,23},{5,24},{6,25},{7,26},{8,27},{9,... | collective-permute-start | bytes 49160
  1280.2 65.7 %collective-permute-start.19 = (f32[16,256]{1,0:T(8,128)S(1)}, f32[16,256]{1,0:T(8,128)S(1)}, u32[]{:S(2)}, u32[]{:S(2)}) collective-permute-start(f32[16,256]{1,0:T(8,128)S(1)} %fusion), channel_id=1, source_target_pairs={{0,20},{1,21},{2,22},{3,23},{4,24},{5,25},{6,26},{7,27},{8,28},{9,... | collective-permute-start | bytes 49160
  1293.3 65.7 %collective-permute-start.2 = (f32[16,256]{1,0:T(8,128)S(1)}, f32[16,256]{1,0:T(8,128)S(1)}, u32[]{:S(2)}, u32[]{:S(2)}) collective-permute-start(f32[16,256]{1,0:T(8,128)S(1)} %fusion), channel_id=1, source_target_pairs={{0,3},{1,4},{2,5},{3,6},{4,7},{5,8},{6,9},{7,10},{8,11},{9,12},{10... | collective-permute-start | bytes 49160
  1306.5 65.7 %collective-permute-start.20 = (f32[16,256]{1,0:T(8,128)S(1)}, f32[16,256]{1,0:T(8,128)S(1)}, u32[]{:S(2)}, u32[]{:S(2)}) collective-permute-start(f32[16,256]{1,0:T(8,128)S(1)} %fusion), channel_id=1, source_target_pairs={{0,21},{1,22},{2,23},{3,24},{4,25},{5,26},{6,27},{7,28},{8,29},{9,... | collective-permute-start | bytes 49160
  1319.6 65.7 %collective-permute-start.21 = (f32[16,256]{1,0:T(8,128)S(1)}, f32[16,256]{1,0:T(8,128)S(1)}, u32[]{:S(2)}, u32[]{:S(2)}) collective-permute-start(f32[16,256]{1,0:T(8,128)S(1)} %fusion), channel_id=1, source_target_pairs={{0,22},{1,23},{2,24},{3,25},{4,26},{5,27},{6,28},{7,29},{8,30},{9,... | collective-permute-start | bytes 49160
  1332.7 65.7 %collective-permute-start.22 = (f32[16,256]{1,0:T(8,128)S(1)}, f32[16,256]{1,0:T(8,128)S(1)}, u32[]{:S(2)}, u32[]{:S(2)}) collective-permute-start(f32[16,256]{1,0:T(8,128)S(1)} %fusion), channel_id=1, source_target_pairs={{0,23},{1,24},{2,25},{3,26},{4,27},{5,28},{6,29},{7,30},{8,31},{9,... | collective-permute-start | bytes 49160
  1345.9 65.7 %collective-permute-start.23 = (f32[16,256]{1,0:T(8,128)S(1)}, f32[16,256]{1,0:T(8,128)S(1)}, u32[]{:S(2)}, u32[]{:S(2)}) collective-permute-start(f32[16,256]{1,0:T(8,128)S(1)} %fusion), channel_id=1, source_target_pairs={{0,24},{1,25},{2,26},{3,27},{4,28},{5,29},{6,30},{7,31},{8,32},{9,... | collective-permute-start | bytes 49160
  1359.0 58.7 %collective-permute-start.24 = (f32[16,256]{1,0:T(8,128)S(1)}, f32[16,256]{1,0:T(8,128)S(1)}, u32[]{:S(2)}, u32[]{:S(2)}) collective-permute-start(f32[16,256]{1,0:T(8,128)S(1)} %fusion), channel_id=1, source_target_pairs={{0,25},{1,26},{2,27},{3,28},{4,29},{5,30},{6,31},{7,32},{8,33},{9,... | collective-permute-start | bytes 49160
  1372.2 50.6 %collective-permute-start.25 = (f32[16,256]{1,0:T(8,128)S(1)}, f32[16,256]{1,0:T(8,128)S(1)}, u32[]{:S(2)}, u32[]{:S(2)}) collective-permute-start(f32[16,256]{1,0:T(8,128)S(1)} %fusion), channel_id=1, source_target_pairs={{0,26},{1,27},{2,28},{3,29},{4,30},{5,31},{6,32},{7,33},{8,34},{9,... | collective-permute-start | bytes 49160
  1385.3 46.2 %collective-permute-start.26 = (f32[16,256]{1,0:T(8,128)S(1)}, f32[16,256]{1,0:T(8,128)S(1)}, u32[]{:S(2)}, u32[]{:S(2)}) collective-permute-start(f32[16,256]{1,0:T(8,128)S(1)} %fusion), channel_id=1, source_target_pairs={{0,27},{1,28},{2,29},{3,30},{4,31},{5,32},{6,33},{7,34},{8,35},{9,... | collective-permute-start | bytes 49160
  1398.4 40.1 %collective-permute-start.27 = (f32[16,256]{1,0:T(8,128)S(1)}, f32[16,256]{1,0:T(8,128)S(1)}, u32[]{:S(2)}, u32[]{:S(2)}) collective-permute-start(f32[16,256]{1,0:T(8,128)S(1)} %fusion), channel_id=1, source_target_pairs={{0,28},{1,29},{2,30},{3,31},{4,32},{5,33},{6,34},{7,35},{8,36},{9,... | collective-permute-start | bytes 49160
  (65 other events, 1042.7 us)
Sparse Core Ops, SparseCore 0:
  9.8 124.8 all-gather.1
  469.4 280.4 all-reduce.38
